TPU v7x, 256 devices: a whole 4x4x8 slice. The times are simulated.
256 devices in a mesh: tm: 8 (over z), height: 16 (over x, y), width: 2 (over core).
Axes of the slice: x: 4, y: 4, z: 8, core: 2. Of those that a mesh axis runs over, the one named last changes fastest.
Arguments:
- video: bfloat16 [2, 128, 16, 256, 128], P('width', ('tm', 'height')), may hold values from -6 to 6
- out_grad: bfloat16 [2, 128, 16, 256, 128], P('width', None, 'tm', 'height'), may hold values from -6 to 6
- lengths: int32 [4], replicated, may hold values from 1 to 6, 16 in all
- temporal_weight: bfloat16 [3, 128, 128], replicated, may hold values from -0.3125 to 0.3125
- spatial_weight: bfloat16 [3, 3, 128, 128], replicated, may hold values from -0.1875 to 0.1875
Outputs:
- video_grad: bfloat16 [2, 128, 16, 256, 128], P('width', ('tm', 'height'))
- temporal_grad: float32 [3, 128, 128], replicated
- spatial_grad: float32 [3, 3, 128, 128], replicated
Inputs may be any that keep to these rules, and one draw needn't show every extreme that they name: The 4 clips lie end to end in frame order, their lengths sum to 16, and the longest clip has exactly 6 frames.
All inputs are finite; a program needn't handle non-finite values.
Results may differ from a plain program's by a relative error of at most 0.008.
Values may be sent and summed in bfloat16 or wider, within the bound.
A program may use at most 128 MiB of HBM per device.

v0:
```python
import jax
import jax.numpy as jnp
from jax import lax
from jax.sharding import PartitionSpec as P


def with_halo(cells, sides, width):
    for axis, dim in sides:
        count = lax.axis_size(axis)
        ends = count - 1
        head = lax.slice_in_dim(cells, 0, width, axis=dim)
        tail = lax.slice_in_dim(cells, cells.shape[dim] - width, cells.shape[dim], axis=dim)
        cells = jnp.concatenate(
            [
                lax.ppermute(tail, axis, [(i, (i + 1) % count) for i in range(ends)]),
                cells,
                lax.ppermute(head, axis, [((i + 1) % count, i) for i in range(ends)]),
            ],
            axis=dim,
        )
    return cells


def frame_masks(lengths, frames):
    ends = jnp.cumsum(lengths, dtype=jnp.int32)
    starts = ends - lengths
    frame_index = jnp.arange(frames, dtype=jnp.int32)
    inside = (frame_index[:, None] >= starts[None, :]) & (frame_index[:, None] < ends[None, :])
    first = jnp.sum(jnp.where(inside, starts[None, :], 0), axis=1, dtype=jnp.int32)
    return jnp.stack([frame_index - lag >= first for lag in range(3)]).astype(jnp.bfloat16)


def silu_slope(pre, grads):
    sig = jax.nn.sigmoid(pre)
    return grads.astype(jnp.float32) * sig * (1.0 + pre * (1.0 - sig))


def flatten(block):
    return block.reshape(-1, block.shape[-1])


def spatial_forward(padded, weights, cols, rows):
    total = None
    for row_off in range(3):
        for col_off in range(3):
            piece = flatten(padded[col_off : col_off + cols, :, row_off : row_off + rows])
            term = jnp.dot(piece, weights[row_off, col_off], preferred_element_type=jnp.float32)
            total = term if total is None else total + term
    return total


def shards(video, out_grad, lengths, temporal_weight, spatial_weight):
    width_loc = video.shape[1]
    frames = video.shape[2]
    rows = video.shape[3]
    chans = video.shape[4]
    n_tm = lax.axis_size("tm")
    n_height = lax.axis_size("height")
    frames_dev = frames // n_tm
    rows_dev = rows // n_height
    cols_half = out_grad.shape[1]
    total_cols = cols_half * lax.axis_size("width")
    masks = frame_masks(lengths, frames)
    local_video = video[0]
    padded_video = jnp.pad(local_video, ((0, 0), (2, 0), (0, 0), (0, 0)))
    taps = [
        padded_video[:, 2 - lag : 2 - lag + frames] * masks[lag][None, :, None, None]
        for lag in range(3)
    ]
    total = None
    for lag in range(3):
        term = jnp.dot(flatten(taps[lag]), temporal_weight[lag], preferred_element_type=jnp.float32)
        total = term if total is None else total + term
    act_time = total.astype(jnp.bfloat16).reshape(local_video.shape)
    arranged = act_time.reshape(width_loc, n_tm, frames_dev, n_height, rows_dev, chans)
    arranged = arranged.transpose(1, 3, 0, 2, 4, 5).reshape(
        n_tm * n_height * width_loc, frames_dev, rows_dev, chans
    )
    act_space = lax.all_to_all(arranged, ("tm", "height"), split_axis=0, concat_axis=0, tiled=True)
    grad_space = out_grad[0]
    padded_act = with_halo(act_space, (("height", 2), ("width", 0)), 1)
    pre = spatial_forward(padded_act, spatial_weight, cols_half, rows_dev)
    delta = silu_slope(pre, flatten(grad_space)).astype(jnp.bfloat16).reshape(act_space.shape)
    padded_delta = with_halo(delta, (("height", 2), ("width", 0)), 1)
    flat_delta = flatten(delta)
    back = None
    spatial_terms = []
    for row_off in range(3):
        line = []
        for col_off in range(3):
            piece = flatten(
                padded_delta[
                    2 - col_off : 2 - col_off + cols_half, :, 2 - row_off : 2 - row_off + rows_dev
                ]
            )
            term = jnp.dot(
                piece, spatial_weight[row_off, col_off].T, preferred_element_type=jnp.float32
            )
            back = term if back is None else back + term
            source = flatten(
                padded_act[col_off : col_off + cols_half, :, row_off : row_off + rows_dev]
            )
            line.append(
                lax.dot_general(
                    source, flat_delta, (((0,), (0,)), ((), ())), preferred_element_type=jnp.float32
                )
            )
        spatial_terms.append(jnp.stack(line))
    spatial_local = jnp.stack(spatial_terms)
    grad_act_space = back.astype(jnp.bfloat16).reshape(act_space.shape)
    received = lax.all_to_all(
        grad_act_space, ("tm", "height"), split_axis=0, concat_axis=0, tiled=True
    )
    received = received.reshape(n_tm, n_height, width_loc, frames_dev, rows_dev, chans)
    grad_time = received.transpose(2, 0, 3, 1, 4, 5).reshape(width_loc, frames, rows, chans)
    flat_grad = flatten(grad_time)
    frame_total = None
    temporal_terms = []
    for lag in range(3):
        temporal_terms.append(
            lax.dot_general(
                flatten(taps[lag]),
                flat_grad,
                (((0,), (0,)), ((), ())),
                preferred_element_type=jnp.float32,
            )
        )
        masked = flatten(grad_time * masks[lag][None, :, None, None])
        product = jnp.dot(
            masked, temporal_weight[lag].T, preferred_element_type=jnp.float32
        ).reshape(grad_time.shape)
        moved = jnp.pad(product[:, lag:], ((0, 0), (0, lag), (0, 0), (0, 0)))
        frame_total = moved if frame_total is None else frame_total + moved
    temporal_local = jnp.stack(temporal_terms)
    video_grad = frame_total.astype(jnp.bfloat16)[None]
    scale = float(frames * rows * total_cols) ** (-0.5)
    temporal_grad, spatial_grad = lax.psum(
        (temporal_local * scale, spatial_local * scale), ("tm", "height", "width")
    )
    return (video_grad, temporal_grad, spatial_grad)


def solution(mesh):
    placed = (
        P("width", ("tm", "height"), None, None, None),
        P("width", None, "tm", "height", None),
        P(),
        P(),
        P(),
    )
    return jax.shard_map(
        shards,
        mesh=mesh,
        in_specs=placed,
        out_specs=(P("width", ("tm", "height"), None, None, None), P(), P()),
        check_vma=False,
    )
```

profile of v0, /device:TPU:2, one launch (start us, length us, event | category | flops | bytes accessed | tf_op | source)
XLA Modules:
  0.0 414.0 jit_solution(14738831127467204281)
XLA Ops:
  8.8 1.4 broadcast_multiply_fusion
  14.0 46.1 %all_to_all.10 = bf16[128,2,16,128]{3,2,1,0:T(8,128)(2,1)S(1)} all-to-all(bf16[128,2,16,128]{3,2,1,0:T(8,128)(2,1)S(1)} %bitcast.249), channel_id=1, replica_groups=mesh['tm'=8,'height'=16,'width'=2] {'tm','height'}, dimensions={0} | all-to-all | bytes 2097152 | tf_op jit(solution)/shard_map/all_to_all | solution.py:79
  60.2 2.4 collective-permute-start
  62.7 5.5 %collective-permute-start.1 = (bf16[128,2,1,128]{3,2,1,0:T(2,128)(2,1)S(1)}, bf16[128,2,1,128]{3,2,1,0:T(2,128)(2,1)S(1)}, u32[]{:S(2)}, u32[]{:S(2)}) collective-permute-start(bf16[128,2,1,128]{3,2,1,0:T(2,128)(2,1)S(1)} %get-tuple-element.38), channel_id=1, source_target_pairs={{2,0},{4,2},{6,4},{8,6},{10,8},{12,10},{14,12},{16,14},{18,16},{20... | collective-permute-start | bytes 196616 | tf_op jit(solution)/shard_map/ppermute | solution.py:17
  69.2 1.5 collective-permute-done.1
  75.1 2.0 maximum_maximum_fusion
  77.1 1.3 fusion.67
  84.4 1.9 collective-permute-start.4
  86.4 6.6 %collective-permute-start.5 = (bf16[128,2,1,128]{3,2,1,0:T(2,128)(2,1)S(1)}, bf16[128,2,1,128]{3,2,1,0:T(2,128)(2,1)S(1)}, u32[]{:S(2)}, u32[]{:S(2)}) collective-permute-start(bf16[128,2,1,128]{3,2,1,0:T(2,128)(2,1)S(1)} %get-tuple-element.34), channel_id=1, source_target_pairs={{2,0},{4,2},{6,4},{8,6},{10,8},{12,10},{14,12},{16,14},{18,16},{20... | collective-permute-start | bytes 196616 | tf_op jit(solution)/shard_map/ppermute | solution.py:17
  93.5 1.6 collective-permute-done.4
  95.1 1.5 collective-permute-done.5
  96.6 1.3 collective-permute-start.6
  97.9 3.0 collective-permute-start.7
  102.4 2.0 pad_maximum_fusion.1
  108.8 1.4 fusion.3
  110.2 10.4 %all-to-all-start.1 = ((bf16[128,2,16,128]{3,2,1,0:T(8,128)(2,1)}), bf16[128,2,16,128]{3,2,1,0:T(8,128)(2,1)}, u32[]{:S(2)}, u32[]{:S(2)}) async-start(bf16[128,2,16,128]{3,2,1,0:T(8,128)(2,1)} %bitcast.251), calls=%async_computation.1 | async-start | bytes 2097152 | tf_op jit(solution)/shard_map/all_to_all | solution.py:111
  120.9 1.8 convolution_bitcast_fusion.10
  127.7 23.3 %all-to-all-done.1 = bf16[128,2,16,128]{3,2,1,0:T(8,128)(2,1)} async-done(((bf16[128,2,16,128]{3,2,1,0:T(8,128)(2,1)}), bf16[128,2,16,128]{3,2,1,0:T(8,128)(2,1)}, u32[]{:S(2)}, u32[]{:S(2)}) %all-to-all-start.1) | async-done | bytes 1048608 | tf_op jit(solution)/shard_map/all_to_all | solution.py:111
  150.9 1.5 copy.12
  154.9 1.5 bitcast_multiply_fusion.2
  157.6 1.4 fusion.8
  159.1 244.5 %all-reduce.6.cloned.1.call-done = (f32[3,128,128]{2,1,0:T(8,128)}, f32[3,3,128,128]{3,2,1,0:T(8,128)}) async-done(((f32[3,128,128]{2,1,0:T(8,128)}, f32[3,3,128,128]{3,2,1,0:T(8,128)}), (f32[3,128,128]{2,1,0:T(8,128)}, f32[3,3,128,128]{3,2,1,0:T(8,128)})) %all-reduce.6.cloned.1.call-update) | async-done | bytes 786448 | tf_op jit(solution)/shard_map/psum | solution.py:137
  403.6 1.6 copy.18
  405.2 1.9 copy.19
  (110 shorter events, 31.7 us)
Async XLA Ops:
  7.2 3.1 copy-start.19
  10.2 1.8 copy-start.9
  10.2 1.6 copy-start.15
  60.2 9.0 %collective-permute-start = (bf16[128,2,1,128]{3,2,1,0:T(2,128)(2,1)S(1)}, bf16[128,2,1,128]{3,2,1,0:T(2,128)(2,1)S(1)}, u32[]{:S(2)}, u32[]{:S(2)}) collective-permute-start(bf16[128,2,1,128]{3,2,1,0:T(2,128)(2,1)S(1)} %get-tuple-element.37), channel_id=1, source_target_pairs={{0,2},{2,4},{4,6},{6,8},{8,10},{10,12},{12,14},{14,16},{16,18},{18... | collective-permute-start | bytes 196616 | tf_op jit(solution)/shard_map/ppermute | solution.py:15
  62.7 8.0 %collective-permute-start.1 = (bf16[128,2,1,128]{3,2,1,0:T(2,128)(2,1)S(1)}, bf16[128,2,1,128]{3,2,1,0:T(2,128)(2,1)S(1)}, u32[]{:S(2)}, u32[]{:S(2)}) collective-permute-start(bf16[128,2,1,128]{3,2,1,0:T(2,128)(2,1)S(1)} %get-tuple-element.38), channel_id=1, source_target_pairs={{2,0},{4,2},{6,4},{8,6},{10,8},{12,10},{14,12},{16,14},{18,16},{20... | collective-permute-start | bytes 196616 | tf_op jit(solution)/shard_map/ppermute | solution.py:17
  68.5 5.9 %copy-start.18 = (bf16[3,3,128,128]{3,2,1,0:T(8,128)(2,1)S(1)}, bf16[3,3,128,128]{3,2,1,0:T(8,128)(2,1)}, u32[]{:S(2)}) copy-start(bf16[3,3,128,128]{3,2,1,0:T(8,128)(2,1)} %param.9) | copy-start | bytes 884740
  70.7 4.1 collective-permute-start.2
  72.0 3.1 collective-permute-start.3
  74.4 8.0 %copy-start.16 = (bf16[128,2,16,128]{3,2,1,0:T(8,128)(2,1)}, bf16[128,2,16,128]{3,2,1,0:T(8,128)(2,1)S(1)}, u32[]{:S(2)}) copy-start(bf16[128,2,16,128]{3,2,1,0:T(8,128)(2,1)S(1)} %get-tuple-element.35) | copy-start | bytes 3145732
  78.5 1.4 copy-start.8
  78.5 1.8 copy-start.6
  78.5 2.2 copy-start.2
  78.5 3.0 copy-start.4
  84.4 10.6 %collective-permute-start.4 = (bf16[128,2,1,128]{3,2,1,0:T(2,128)(2,1)S(1)}, bf16[128,2,1,128]{3,2,1,0:T(2,128)(2,1)S(1)}, u32[]{:S(2)}, u32[]{:S(2)}) collective-permute-start(bf16[128,2,1,128]{3,2,1,0:T(2,128)(2,1)S(1)} %get-tuple-element.33), channel_id=1, source_target_pairs={{0,2},{2,4},{4,6},{6,8},{8,10},{10,12},{12,14},{14,16},{16,18},{18... | collective-permute-start | bytes 196616 | tf_op jit(solution)/shard_map/ppermute | solution.py:15
  86.4 10.2 %collective-permute-start.5 = (bf16[128,2,1,128]{3,2,1,0:T(2,128)(2,1)S(1)}, bf16[128,2,1,128]{3,2,1,0:T(2,128)(2,1)S(1)}, u32[]{:S(2)}, u32[]{:S(2)}) collective-permute-start(bf16[128,2,1,128]{3,2,1,0:T(2,128)(2,1)S(1)} %get-tuple-element.34), channel_id=1, source_target_pairs={{2,0},{4,2},{6,4},{8,6},{10,8},{12,10},{14,12},{16,14},{18,16},{20... | collective-permute-start | bytes 196616 | tf_op jit(solution)/shard_map/ppermute | solution.py:17
  96.6 5.8 %collective-permute-start.6 = (bf16[1,2,18,128]{3,2,1,0:T(8,128)(2,1)S(1)}, bf16[1,2,18,128]{3,2,1,0:T(8,128)(2,1)S(1)}, u32[]{:S(2)}, u32[]{:S(2)}) collective-permute-start(bf16[1,2,18,128]{3,2,1,0:T(8,128)(2,1)S(1)} %get-tuple-element.22), channel_id=1, source_target_pairs={{1,0},{3,2},{5,4},{7,6},{9,8},{11,10},{13,12},{15,14},{17,16},{19,... | collective-permute-start | bytes 27656 | tf_op jit(solution)/shard_map/ppermute | solution.py:17
  97.9 4.5 %collective-permute-start.7 = (bf16[1,2,18,128]{3,2,1,0:T(8,128)(2,1)S(1)}, bf16[1,2,18,128]{3,2,1,0:T(8,128)(2,1)S(1)}, u32[]{:S(2)}, u32[]{:S(2)}) collective-permute-start(bf16[1,2,18,128]{3,2,1,0:T(8,128)(2,1)S(1)} %get-tuple-element.23), channel_id=1, source_target_pairs={{0,1},{2,3},{4,5},{6,7},{8,9},{10,11},{12,13},{14,15},{16,17},{18,... | collective-permute-start | bytes 27656 | tf_op jit(solution)/shard_map/ppermute | solution.py:15
  110.2 40.7 %all-to-all-start.1 = ((bf16[128,2,16,128]{3,2,1,0:T(8,128)(2,1)}), bf16[128,2,16,128]{3,2,1,0:T(8,128)(2,1)}, u32[]{:S(2)}, u32[]{:S(2)}) async-start(bf16[128,2,16,128]{3,2,1,0:T(8,128)(2,1)} %bitcast.251), calls=%async_computation.1 | async-start | bytes 2097152 | tf_op jit(solution)/shard_map/all_to_all | solution.py:111
  120.6 282.9 %all-reduce.6.cloned.1.call-start = ((), (), s32[]{:S(2)}) async-start(), calls=%async_computation.2 | async-start | bytes 1572864 | tf_op jit(solution)/shard_map/psum | solution.py:137
  120.9 1.9 copy-start.7
  120.9 2.4 copy-start.5
  124.5 1.3 copy-start.1
  126.8 25.7 %copy-start.14 = (bf16[1,16,256,128]{3,2,1,0:T(8,128)(2,1)S(1)}, bf16[1,16,256,128]{3,2,1,0:T(8,128)(2,1)}, u32[]{:S(2)}) copy-start(bf16[1,16,256,128]{3,2,1,0:T(8,128)(2,1)} %copy-done.13) | copy-start | bytes 3145732
  150.9 2.0 copy-start.12
  (7 other events, 8.2 us)
Sparse Core Ops, SparseCore 0:
  155.1 248.4 all-reduce.5
where the time goes:
time: 415 us; the launch traced here: 414 us
  waiting for transfers between devices  273 us (66%)
  blocking collectives  46.1 us (11%)
  starting transfers between devices  34.1 us (8%)
  matrix products  20 us (5%)
  between operations  14.7 us (4%)
  local copies, waits for them, and re-layouts  13.4 us (3%)
  other arithmetic  12.4 us (3%)
    psum x1, waiting for transfers between devices, shards(): lax.psum((temporal_local * scale, spatial_local * scale), ('tm', 'height'...  245 us
    all_to_all x1, blocking collectives, shards(): lax.all_to_all(arranged, ('tm', 'height'), split_axis=0, concat_axis=0, t...  46.1 us
    all_to_all x1, waiting for transfers between devices, shards(): lax.all_to_all(grad_act_space, ('tm', 'height'), split_axis=0, concat_axi...  23.3 us
    ppermute x4, starting transfers between devices, with_halo(): lax.ppermute(head, axis, [((i + 1) % count, i) for i in range(ends)])  14.7 us
    all_to_all x1, starting transfers between devices, shards(): lax.all_to_all(grad_act_space, ('tm', 'height'), split_axis=0, concat_axi...  10.4 us
    ppermute x4, starting transfers between devices, with_halo(): lax.ppermute(tail, axis, [(i, (i + 1) % count) for i in range(ends)])  8.68 us
  transfers between devices with their start and end apart: 10, of which 7 were waited for; matrix products, arithmetic and copies ran while one was open for 3% of the time, Pallas kernels for 0%

commit v1 on v0

--- a/solution.py
+++ b/solution.py
@@ -2,6 +2,7 @@
 import jax.numpy as jnp
 from jax import lax
 from jax.sharding import PartitionSpec as P
+from jax.lax import psum
 
 
 def with_halo(cells, sides, width):
@@ -134,8 +135,8 @@
     temporal_local = jnp.stack(temporal_terms)
     video_grad = frame_total.astype(jnp.bfloat16)[None]
     scale = float(frames * rows * total_cols) ** (-0.5)
-    temporal_grad, spatial_grad = lax.psum(
-        (temporal_local * scale, spatial_local * scale), ("tm", "height", "width")
+    temporal_grad, spatial_grad = psum(
+        psum((temporal_local * scale, spatial_local * scale), "tm"), ("height", "width")
     )
     return (video_grad, temporal_grad, spatial_grad)
 

time: 415 us -> 352 us (0.85)
  waiting for transfers between devices: 273 us -> 209 us
    psum x1 -> x2, waiting for transfers between devices: 245 us -> 180 us  [the longest x1 113 us: shards(): psum(psum((temporal_local * scale, spatial_local * scale), 'tm'), ('heigh...]
  transfers between devices with their start and end apart: 10 -> 11, of which waited for: 7 -> 8; matrix products, arithmetic and copies ran while one was open for 3% -> 4% of each run, Pallas kernels for 0% -> 0%
where the time goes in v1:
time: 352 us; the launch traced here: 350 us
  waiting for transfers between devices  209 us (59%)
  blocking collectives  46.1 us (13%)
  starting transfers between devices  34.3 us (10%)
  matrix products  19.9 us (6%)
  between operations  14.7 us (4%)
  local copies, waits for them, and re-layouts  13.5 us (4%)
  other arithmetic  12.4 us (4%)
    psum x1, waiting for transfers between devices, shards(): psum(psum((temporal_local * scale, spatial_local * scale), 'tm'), ('heigh...  113 us
    psum x1, waiting for transfers between devices, shards(): psum((temporal_local * scale, spatial_local * scale), 'tm')  67 us
    all_to_all x1, blocking collectives, shards(): lax.all_to_all(arranged, ('tm', 'height'), split_axis=0, concat_axis=0, t...  46.1 us
    all_to_all x1, waiting for transfers between devices, shards(): lax.all_to_all(grad_act_space, ('tm', 'height'), split_axis=0, concat_axi...  23.3 us
    ppermute x4, starting transfers between devices, with_halo(): lax.ppermute(head, axis, [((i + 1) % count, i) for i in range(ends)])  14.9 us
    all_to_all x1, starting transfers between devices, shards(): lax.all_to_all(grad_act_space, ('tm', 'height'), split_axis=0, concat_axi...  10.4 us
    ppermute x4, starting transfers between devices, with_halo(): lax.ppermute(tail, axis, [(i, (i + 1) % count) for i in range(ends)])  8.68 us
    unnamed x44, local copies, waits for them, and re-layouts  8.11 us
  transfers between devices with their start and end apart: 11, of which 8 were waited for; matrix products, arithmetic and copies ran while one was open for 4% of the time, Pallas kernels for 0%

profile of v1, /device:TPU:2, one launch (start us, length us, event | category | flops | bytes accessed | tf_op | source)
XLA Modules:
  0.0 349.8 jit_solution(8325672010279623250)
XLA Ops:
  8.8 1.4 broadcast_multiply_fusion
  14.0 46.1 %all_to_all.10 = bf16[128,2,16,128]{3,2,1,0:T(8,128)(2,1)S(1)} all-to-all(bf16[128,2,16,128]{3,2,1,0:T(8,128)(2,1)S(1)} %bitcast.249), channel_id=1, replica_groups=mesh['tm'=8,'height'=16,'width'=2] {'tm','height'}, dimensions={0} | all-to-all | bytes 2097152 | tf_op jit(solution)/shard_map/all_to_all | solution.py:80
  60.2 2.4 collective-permute-start
  62.7 5.6 %collective-permute-start.1 = (bf16[128,2,1,128]{3,2,1,0:T(2,128)(2,1)S(1)}, bf16[128,2,1,128]{3,2,1,0:T(2,128)(2,1)S(1)}, u32[]{:S(2)}, u32[]{:S(2)}) collective-permute-start(bf16[128,2,1,128]{3,2,1,0:T(2,128)(2,1)S(1)} %get-tuple-element.40), channel_id=1, source_target_pairs={{2,0},{4,2},{6,4},{8,6},{10,8},{12,10},{14,12},{16,14},{18,16},{20... | collective-permute-start | bytes 196616 | tf_op jit(solution)/shard_map/ppermute | solution.py:18
  69.2 1.6 collective-permute-done.1
  75.2 2.0 maximum_maximum_fusion
  77.2 1.3 fusion.67
  84.6 1.9 collective-permute-start.4
  86.5 6.6 %collective-permute-start.5 = (bf16[128,2,1,128]{3,2,1,0:T(2,128)(2,1)S(1)}, bf16[128,2,1,128]{3,2,1,0:T(2,128)(2,1)S(1)}, u32[]{:S(2)}, u32[]{:S(2)}) collective-permute-start(bf16[128,2,1,128]{3,2,1,0:T(2,128)(2,1)S(1)} %get-tuple-element.36), channel_id=1, source_target_pairs={{2,0},{4,2},{6,4},{8,6},{10,8},{12,10},{14,12},{16,14},{18,16},{20... | collective-permute-start | bytes 196616 | tf_op jit(solution)/shard_map/ppermute | solution.py:18
  93.7 1.6 collective-permute-done.4
  95.2 1.5 collective-permute-done.5
  98.1 3.0 collective-permute-start.7
  102.6 2.0 pad_maximum_fusion.1
  108.9 1.4 fusion.3
  110.4 10.4 %all-to-all-start.1 = ((bf16[128,2,16,128]{3,2,1,0:T(8,128)(2,1)}), bf16[128,2,16,128]{3,2,1,0:T(8,128)(2,1)}, u32[]{:S(2)}, u32[]{:S(2)}) async-start(bf16[128,2,16,128]{3,2,1,0:T(8,128)(2,1)} %bitcast.251), calls=%async_computation.1 | async-start | bytes 2097152 | tf_op jit(solution)/shard_map/all_to_all | solution.py:112
  121.1 1.8 convolution_bitcast_fusion.10
  127.8 23.3 %all-to-all-done.1 = bf16[128,2,16,128]{3,2,1,0:T(8,128)(2,1)} async-done(((bf16[128,2,16,128]{3,2,1,0:T(8,128)(2,1)}), bf16[128,2,16,128]{3,2,1,0:T(8,128)(2,1)}, u32[]{:S(2)}, u32[]{:S(2)}) %all-to-all-start.1) | async-done | bytes 1048608 | tf_op jit(solution)/shard_map/all_to_all | solution.py:112
  151.1 1.5 copy.12
  155.4 1.5 bitcast_multiply_fusion.2
  156.9 67.0 %all-reduce.10.cloned.1.call-done = (f32[3,128,128]{2,1,0:T(8,128)}, f32[3,3,128,128]{3,2,1,0:T(8,128)}) async-done(((f32[3,128,128]{2,1,0:T(8,128)}, f32[3,3,128,128]{3,2,1,0:T(8,128)}), (f32[3,128,128]{2,1,0:T(8,128)}, f32[3,3,128,128]{3,2,1,0:T(8,128)})) %all-reduce.10.cloned.1.call-update) | async-done | bytes 786448 | tf_op jit(solution)/shard_map/psum | solution.py:139
  225.1 1.4 fusion.8
  226.5 112.9 %all-reduce.8.cloned.1.call-done = (f32[3,128,128]{2,1,0:T(8,128)}, f32[3,3,128,128]{3,2,1,0:T(8,128)}) async-done(((f32[3,128,128]{2,1,0:T(8,128)}, f32[3,3,128,128]{3,2,1,0:T(8,128)}), (f32[3,128,128]{2,1,0:T(8,128)}, f32[3,3,128,128]{3,2,1,0:T(8,128)})) %all-reduce.8.cloned.1.call-update) | async-done | bytes 786448 | tf_op jit(solution)/shard_map/psum | solution.py:138
  339.4 1.6 copy.20
  341.0 1.9 copy.21
  (113 shorter events, 33.2 us)
Async XLA Ops:
  7.2 3.1 copy-start.19
  10.2 1.8 copy-start.9
  10.2 1.6 copy-start.15
  60.2 9.0 %collective-permute-start = (bf16[128,2,1,128]{3,2,1,0:T(2,128)(2,1)S(1)}, bf16[128,2,1,128]{3,2,1,0:T(2,128)(2,1)S(1)}, u32[]{:S(2)}, u32[]{:S(2)}) collective-permute-start(bf16[128,2,1,128]{3,2,1,0:T(2,128)(2,1)S(1)} %get-tuple-element.39), channel_id=1, source_target_pairs={{0,2},{2,4},{4,6},{6,8},{8,10},{10,12},{12,14},{14,16},{16,18},{18... | collective-permute-start | bytes 196616 | tf_op jit(solution)/shard_map/ppermute | solution.py:16
  62.7 11.8 %copy-start.18 = (bf16[3,3,128,128]{3,2,1,0:T(8,128)(2,1)S(1)}, bf16[3,3,128,128]{3,2,1,0:T(8,128)(2,1)}, u32[]{:S(2)}) copy-start(bf16[3,3,128,128]{3,2,1,0:T(8,128)(2,1)} %param.9) | copy-start | bytes 884740
  62.7 8.1 %collective-permute-start.1 = (bf16[128,2,1,128]{3,2,1,0:T(2,128)(2,1)S(1)}, bf16[128,2,1,128]{3,2,1,0:T(2,128)(2,1)S(1)}, u32[]{:S(2)}, u32[]{:S(2)}) collective-permute-start(bf16[128,2,1,128]{3,2,1,0:T(2,128)(2,1)S(1)} %get-tuple-element.40), channel_id=1, source_target_pairs={{2,0},{4,2},{6,4},{8,6},{10,8},{12,10},{14,12},{16,14},{18,16},{20... | collective-permute-start | bytes 196616 | tf_op jit(solution)/shard_map/ppermute | solution.py:18
  70.9 4.1 %collective-permute-start.2 = (bf16[1,2,18,128]{3,2,1,0:T(8,128)(2,1)S(1)}, bf16[1,2,18,128]{3,2,1,0:T(8,128)(2,1)S(1)}, u32[]{:S(2)}, u32[]{:S(2)}) collective-permute-start(bf16[1,2,18,128]{3,2,1,0:T(8,128)(2,1)S(1)} %get-tuple-element.28), channel_id=1, source_target_pairs={{0,1},{2,3},{4,5},{6,7},{8,9},{10,11},{12,13},{14,15},{16,17},{18,... | collective-permute-start | bytes 27656 | tf_op jit(solution)/shard_map/ppermute | solution.py:16
  72.2 3.1 collective-permute-start.3
  74.5 8.0 %copy-start.16 = (bf16[128,2,16,128]{3,2,1,0:T(8,128)(2,1)}, bf16[128,2,16,128]{3,2,1,0:T(8,128)(2,1)S(1)}, u32[]{:S(2)}) copy-start(bf16[128,2,16,128]{3,2,1,0:T(8,128)(2,1)S(1)} %get-tuple-element.37) | copy-start | bytes 3145732
  78.6 1.4 copy-start.8
  78.6 1.8 copy-start.6
  78.6 2.2 copy-start.2
  78.6 3.0 copy-start.4
  84.6 10.6 %collective-permute-start.4 = (bf16[128,2,1,128]{3,2,1,0:T(2,128)(2,1)S(1)}, bf16[128,2,1,128]{3,2,1,0:T(2,128)(2,1)S(1)}, u32[]{:S(2)}, u32[]{:S(2)}) collective-permute-start(bf16[128,2,1,128]{3,2,1,0:T(2,128)(2,1)S(1)} %get-tuple-element.35), channel_id=1, source_target_pairs={{0,2},{2,4},{4,6},{6,8},{8,10},{10,12},{12,14},{14,16},{16,18},{18... | collective-permute-start | bytes 196616 | tf_op jit(solution)/shard_map/ppermute | solution.py:16
  86.5 10.2 %collective-permute-start.5 = (bf16[128,2,1,128]{3,2,1,0:T(2,128)(2,1)S(1)}, bf16[128,2,1,128]{3,2,1,0:T(2,128)(2,1)S(1)}, u32[]{:S(2)}, u32[]{:S(2)}) collective-permute-start(bf16[128,2,1,128]{3,2,1,0:T(2,128)(2,1)S(1)} %get-tuple-element.36), channel_id=1, source_target_pairs={{2,0},{4,2},{6,4},{8,6},{10,8},{12,10},{14,12},{16,14},{18,16},{20... | collective-permute-start | bytes 196616 | tf_op jit(solution)/shard_map/ppermute | solution.py:18
  96.8 5.8 %collective-permute-start.6 = (bf16[1,2,18,128]{3,2,1,0:T(8,128)(2,1)S(1)}, bf16[1,2,18,128]{3,2,1,0:T(8,128)(2,1)S(1)}, u32[]{:S(2)}, u32[]{:S(2)}) collective-permute-start(bf16[1,2,18,128]{3,2,1,0:T(8,128)(2,1)S(1)} %get-tuple-element.24), channel_id=1, source_target_pairs={{1,0},{3,2},{5,4},{7,6},{9,8},{11,10},{13,12},{15,14},{17,16},{19,... | collective-permute-start | bytes 27656 | tf_op jit(solution)/shard_map/ppermute | solution.py:18
  98.1 4.5 %collective-permute-start.7 = (bf16[1,2,18,128]{3,2,1,0:T(8,128)(2,1)S(1)}, bf16[1,2,18,128]{3,2,1,0:T(8,128)(2,1)S(1)}, u32[]{:S(2)}, u32[]{:S(2)}) collective-permute-start(bf16[1,2,18,128]{3,2,1,0:T(8,128)(2,1)S(1)} %get-tuple-element.25), channel_id=1, source_target_pairs={{0,1},{2,3},{4,5},{6,7},{8,9},{10,11},{12,13},{14,15},{16,17},{18,... | collective-permute-start | bytes 27656 | tf_op jit(solution)/shard_map/ppermute | solution.py:16
  110.4 40.7 %all-to-all-start.1 = ((bf16[128,2,16,128]{3,2,1,0:T(8,128)(2,1)}), bf16[128,2,16,128]{3,2,1,0:T(8,128)(2,1)}, u32[]{:S(2)}, u32[]{:S(2)}) async-start(bf16[128,2,16,128]{3,2,1,0:T(8,128)(2,1)} %bitcast.251), calls=%async_computation.1 | async-start | bytes 2097152 | tf_op jit(solution)/shard_map/all_to_all | solution.py:112
  120.8 103.1 %all-reduce.10.cloned.1.call-start = ((), (), s32[]{:S(2)}) async-start(), calls=%async_computation.3 | async-start | bytes 1572864 | tf_op jit(solution)/shard_map/psum | solution.py:139
  121.1 1.9 copy-start.7
  121.1 2.4 copy-start.5
  126.9 25.7 %copy-start.14 = (bf16[1,16,256,128]{3,2,1,0:T(8,128)(2,1)S(1)}, bf16[1,16,256,128]{3,2,1,0:T(8,128)(2,1)}, u32[]{:S(2)}) copy-start(bf16[1,16,256,128]{3,2,1,0:T(8,128)(2,1)} %copy-done.13) | copy-start | bytes 3145732
  151.1 2.0 copy-start.12
  155.1 184.3 %all-reduce.8.cloned.1.call-start = ((), (), s32[]{:S(2)}) async-start(), calls=%async_computation.2 | async-start | bytes 1572864 | tf_op jit(solution)/shard_map/psum | solution.py:138
  (8 other events, 9.5 us)
Sparse Core Ops, SparseCore 0:
  155.2 68.6 all-reduce.9
  227.5 111.8 all-reduce.7
